TPU v7x, 32 devices: a whole 2x2x4 slice. The times are simulated.
32 devices in a mesh: dp: 8 (over z, y), rep: 4 (over x, core).
Axes of the slice: x: 2, y: 2, z: 4, core: 2. Of those that a mesh axis runs over, the one named last changes fastest.
Arguments:
- circuits: bfloat16 [8192, 1024], P(('dp', 'rep')), may hold values from -2.65 to 2.65
- records: bfloat16 [8192, 1024], P(('dp', 'rep')), may hold values from -0.25 to 0.25
- record_gain: float32 [1024], replicated, may hold values from 0.5 to 2
- log_scale: float32 [1], replicated, may hold values from 1.6 to 2.4
- logit_bias: float32 [1], replicated, may hold values from -3 to -1
- hard_ids: int32 [8192, 16], P(('dp', 'rep')), may hold values from -1 to 8191, as said below
Outputs:
- grad_circuits: float32 [8192, 1024], P(('dp', 'rep'))
- grad_records: float32 [8192, 1024], P(('dp', 'rep'))
- grad_gain: float32 [1024], replicated
- statistics: float32 [2], replicated
- mean_loss: float32 [1], replicated
Inputs may be any that keep to these rules, and one draw needn't show every extreme that they name: `hard_ids`: every entry that is not -1 names a row held by a device with the same dp index as the pair's device (the same value of row // 1024). Over the 256 pairs of one device, at most 16 entries name rows of any one device, and in each dp index one device is named exactly 16 times by every device of that dp index.
All inputs are finite; a program needn't handle non-finite values.
Results may differ from a plain program's by a relative error of at most 0.0043.
Values may be sent and summed in bfloat16 or wider, within the bound.
A program may use at most 64 MiB of HBM per device.

v0:
```python
import jax
import jax.numpy as jnp
from jax import lax
from jax.sharding import PartitionSpec as P

HOPS = 4
CAP = 16
EPSILON = 1e-06


def shifted(value, axis, steps):
    count = lax.axis_size(axis)
    pairs = [(source, (source + steps) % count) for source in range(count)]
    return lax.ppermute(value, axis, pairs)


def unit_rows(values):
    sq_total = jnp.sum(values * values, axis=-1, keepdims=True)
    lengths = jnp.sqrt(sq_total + EPSILON)
    return (values / lengths, lengths)


def transposed_product(left, right):
    return lax.dot_general(
        left, right, (((0,), (0,)), ((), ())), preferred_element_type=jnp.float32
    )


def score_tile(circ_block, rec_block, multiplier, bias_value, own_block):
    products = lax.dot_general(
        circ_block, rec_block, (((1,), (1,)), ((), ())), preferred_element_type=jnp.float32
    )
    scores = products * multiplier + bias_value
    weights = jax.nn.sigmoid(scores)
    losses = jax.nn.softplus(scores)
    if own_block:
        tile_rows = scores.shape[0]
        diag_mask = (
            lax.broadcasted_iota(jnp.int32, (tile_rows, tile_rows), 0)
            == lax.broadcasted_iota(jnp.int32, (tile_rows, tile_rows), 1)
        ).astype(jnp.float32)
        weights = weights - diag_mask
        losses = losses - scores * diag_mask
    summary = jnp.stack(
        [jnp.sum(weights * (scores - bias_value)), jnp.sum(weights), jnp.sum(losses)]
    )
    return (weights.astype(jnp.bfloat16), summary)


def per_device(circuits, records, record_gain, log_scale, logit_bias, hard_ids):
    pair_rows = circuits.shape[0]
    list_width = hard_ids.shape[1]
    rep_count = lax.axis_size("rep")
    loop_count = lax.axis_size("dp")
    circ_unit, circ_length = unit_rows(circuits.astype(jnp.float32))
    circ_emb = circ_unit.astype(jnp.bfloat16)
    rec_pre = records.astype(jnp.float32) * record_gain
    rec_unit, rec_length = unit_rows(rec_pre)
    rec_emb = rec_unit.astype(jnp.bfloat16)
    multiplier = jnp.exp(log_scale[0])
    bias_value = logit_bias[0]
    own_weights, summary = score_tile(circ_emb, rec_emb, multiplier, bias_value, True)
    grad_circ = jnp.dot(own_weights, rec_emb, preferred_element_type=jnp.float32)
    running = transposed_product(own_weights, circ_emb)
    visitor = rec_emb
    for hop_index in range(HOPS):
        visitor = shifted(visitor, "dp", -1)
        running = shifted(running, "dp", -1)
        weights, portion = score_tile(circ_emb, visitor, multiplier, bias_value, False)
        grad_circ = grad_circ + jnp.dot(weights, visitor, preferred_element_type=jnp.float32)
        summary = summary + portion
        running = running + transposed_product(weights, circ_emb)
    grad_rec = shifted(running, "dp", HOPS)
    entry_ids = hard_ids.reshape(-1)
    entry_count = entry_ids.shape[0]
    is_live = entry_ids >= 0
    owner_dev = entry_ids // pair_rows % rep_count
    row_within = entry_ids % pair_rows
    owner_hits = (
        (owner_dev[:, None] == jnp.arange(rep_count, dtype=jnp.int32)[None, :]) & is_live[:, None]
    ).astype(jnp.int32)
    before = jnp.cumsum(owner_hits, axis=0) - owner_hits
    slot_index = jnp.sum(before * owner_hits, axis=1)
    slot_total = rep_count * CAP
    target = jnp.where(is_live, owner_dev * CAP + slot_index, slot_total)
    asked_rows = (
        jnp.zeros((slot_total,), jnp.int32)
        .at[target]
        .set(row_within, mode="drop")
        .reshape(rep_count, CAP)
    )
    slot_pair = (
        jnp.zeros((slot_total,), jnp.int32)
        .at[target]
        .set(jnp.arange(entry_count, dtype=jnp.int32) // list_width, mode="drop")
    )
    slot_live = jnp.zeros((slot_total,), jnp.float32).at[target].set(1.0, mode="drop")
    found_rows = jnp.take(
        rec_emb, lax.all_to_all(asked_rows, "rep", split_axis=0, concat_axis=0, tiled=True), axis=0
    )
    fetched = lax.all_to_all(found_rows, "rep", split_axis=0, concat_axis=0, tiled=True)
    fetched = fetched.reshape(slot_total, fetched.shape[2])
    slot_products = lax.dot_general(
        fetched, circ_emb, (((1,), (1,)), ((), ())), preferred_element_type=jnp.float32
    )
    chosen = (slot_pair[:, None] == lax.broadcasted_iota(jnp.int32, (slot_total, pair_rows), 1)) & (
        slot_live[:, None] > 0
    )
    hard_products = jnp.sum(jnp.where(chosen, slot_products, 0.0), axis=1)
    hard_scores = hard_products * multiplier + bias_value
    hard_weights = jnp.where(slot_live > 0, jax.nn.sigmoid(hard_scores), 0.0)
    hard_losses = jnp.where(slot_live > 0, jax.nn.softplus(hard_scores), 0.0)
    spread = jnp.where(
        chosen, hard_weights.astype(jnp.bfloat16)[:, None], jnp.zeros((), jnp.bfloat16)
    )
    hard_grad = transposed_product(spread, fetched)
    summary = summary + jnp.stack(
        [
            jnp.sum(hard_weights * hard_products * multiplier),
            jnp.sum(hard_weights),
            jnp.sum(hard_losses),
        ]
    )
    grad_circ_emb = multiplier * (grad_circ + hard_grad)
    grad_rec_emb = multiplier * grad_rec
    grad_circuits = (
        grad_circ_emb - circ_unit * jnp.sum(circ_unit * grad_circ_emb, axis=-1, keepdims=True)
    ) / circ_length
    grad_pre = (
        grad_rec_emb - rec_unit * jnp.sum(rec_unit * grad_rec_emb, axis=-1, keepdims=True)
    ) / rec_length
    grad_records = grad_pre * record_gain
    gain_part = jnp.sum(records.astype(jnp.float32) * grad_pre, axis=0)
    gain_total, summary_total = lax.psum((gain_part, summary), ("dp", "rep"))
    pair_total = pair_rows * loop_count * rep_count
    statistics = jnp.stack([summary_total[0], summary_total[1]])
    mean_loss = jnp.stack([summary_total[2] / pair_total])
    return (grad_circuits, grad_records, gain_total, statistics, mean_loss)


def solution(mesh):
    placed = (P(("dp", "rep"), None), P(("dp", "rep"), None), P(), P(), P(), P(("dp", "rep"), None))
    return jax.shard_map(
        per_device,
        mesh=mesh,
        in_specs=placed,
        out_specs=(P(("dp", "rep"), None), P(("dp", "rep"), None), P(), P(), P()),
        check_vma=False,
    )
```

profile of v0, /device:TPU:12, one launch (start us, length us, event | category | flops | bytes accessed | tf_op | source)
XLA Modules:
  0.0 262.5 jit_solution(4319335786389604963)
XLA Ops:
  0.6 0.8 copy.14
  1.9 1.2 reduce-window.6
  3.1 0.2 slice_reduce_fusion
  3.3 0.2 reduce-window.9
  3.9 15.5 %scatter_custom_fusion.2 = s32[64]{0:T(128)S(1)} fusion(s32[4096]{0:T(1024)S(1)} %bitcast.84, s32[4096]{0:T(1024)S(1)} %get-tuple-element.28, s32[]{:T(128)} %constant.87.clone.1), kind=kCustom, calls=%fused_computation.158 | custom fusion | bytes 260 | tf_op jit(solution)/shard_map/scatter | solution.py:89
  19.4 0.7 all_to_all.13
  20.0 3.2 %all-to-all-start = ((s32[4,1,16]{2,1,0:T(1,128)}), s32[4,1,16]{2,1,0:T(1,128)S(1)}, u32[]{:S(2)}, u32[]{:S(2)}) async-start(s32[4,1,16]{2,1,0:T(1,128)} %bitcast.5), calls=%async_computation | async-start | bytes 4096 | tf_op jit(solution)/shard_map/all_to_all | solution.py:99
  23.3 0.2 fusion.10
  23.7 0.6 collective-permute-start
  24.3 0.3 copy-done.1
  24.6 0.2 fusion.11
  24.8 0.2 fusion.72
  26.3 1.2 multiply_reduce_fusion.6
  27.6 1.3 fusion.33
  28.9 1.1 collective-permute-start.4
  30.0 15.5 %scatter_custom_fusion.1 = f32[64]{0:T(128)S(1)} fusion(s32[4096]{0:T(1024)S(1)} %bitcast.85, f32[4096]{0:T(1024)S(1)} %broadcast.271, f32[]{:T(128)} %constant.85.clone.1), kind=kCustom, calls=%fused_computation.156 | custom fusion | bytes 260 | tf_op jit(solution)/shard_map/scatter | solution.py:97
  45.5 0.3 fusion.35
  45.8 0.2 copy-done.5
  46.0 0.5 broadcast_compare_fusion.2
  46.5 16.0 %scatter_custom_fusion = s32[64]{0:T(128)} fusion(s32[4096]{0:T(1024)S(1)} %bitcast.86, s32[4096]{0:T(1024)S(1)} %add_select_fusion.1, s32[]{:T(128)} %constant.87.clone.1), kind=kCustom, calls=%fused_computation.160 | custom fusion | bytes 260 | tf_op jit(solution)/shard_map/scatter | solution.py:95
  62.6 0.8 collective-permute-start.1
  63.4 2.3 multiply_reduce_fusion.5
  65.7 2.5 convolution_add_fusion
  68.3 4.3 %collective-permute-start.5 = (f32[256,1024]{1,0:T(8,128)}, f32[256,1024]{1,0:T(8,128)}, u32[]{:S(2)}, u32[]{:S(2)}) collective-permute-start(f32[256,1024]{1,0:T(8,128)} %convolution_add_fusion), channel_id=1, source_target_pairs={{0,28},{4,0},{8,4},{12,8},{16,12},{20,16},{24,20},{28,24},{1,29},{... | collective-permute-start | bytes 3145736 | tf_op jit(solution)/shard_map/ppermute | solution.py:14
  72.5 0.6 pad_clamp_fusion
  73.1 0.8 gather_fusion
  74.0 0.7 broadcast_select_fusion
  74.7 3.3 %all-to-all-start.1 = ((bf16[4,16,1024]{2,1,0:T(8,128)(2,1)}), bf16[4,16,1024]{2,1,0:T(8,128)(2,1)S(1)}, u32[]{:S(2)}, u32[]{:S(2)}) async-start(bf16[4,16,1024]{2,1,0:T(8,128)(2,1)} %broadcast_select_fusion), calls=%async_computation.1 | async-start | bytes 262144 | tf_op jit(solution)/shard_map/all_to_all | solution.py:101
  78.0 0.6 collective-permute-done.1
  78.6 2.3 multiply_reduce_fusion.4
  80.9 0.3 fusion.28
  81.2 1.7 collective-permute-start.2
  83.0 18.1 %collective-permute-done.5 = f32[256,1024]{1,0:T(8,128)} collective-permute-done((f32[256,1024]{1,0:T(8,128)}, f32[256,1024]{1,0:T(8,128)}, u32[]{:S(2)}, u32[]{:S(2)}) %collective-permute-start.5) | collective-permute-done | bytes 1048608 | tf_op jit(solution)/shard_map/ppermute | solution.py:14
  101.1 2.3 add.241
  103.4 1.7 collective-permute-start.6
  105.1 0.4 fusion.9
  105.5 0.6 copy-done.6
  106.1 0.6 multiply_reduce_fusion.7
  106.8 0.4 fusion.42
  107.2 5.2 %collective-permute-done.2 = bf16[256,1024]{1,0:T(8,128)(2,1)} collective-permute-done((bf16[256,1024]{1,0:T(8,128)(2,1)}, bf16[256,1024]{1,0:T(8,128)(2,1)}, u32[]{:S(2)}, u32[]{:S(2)}) %collective-permute-start.2) | collective-permute-done | bytes 524320 | tf_op jit(solution)/shard_map/ppermute | solution.py:14
  112.3 1.7 collective-permute-start.3
  114.0 2.2 multiply_reduce_fusion.3
  116.3 0.3 fusion.25
  116.6 18.2 %collective-permute-done.6 = f32[256,1024]{1,0:T(8,128)} collective-permute-done((f32[256,1024]{1,0:T(8,128)}, f32[256,1024]{1,0:T(8,128)}, u32[]{:S(2)}, u32[]{:S(2)}) %collective-permute-start.6) | collective-permute-done | bytes 1048608 | tf_op jit(solution)/shard_map/ppermute | solution.py:14
  134.8 1.4 add.242
  136.2 1.9 collective-permute-start.7
  138.1 1.4 convolution_add_fusion.4
  139.4 1.4 convolution_add_fusion.3
  140.8 5.1 %collective-permute-done.3 = bf16[256,1024]{1,0:T(8,128)(2,1)S(1)} collective-permute-done((bf16[256,1024]{1,0:T(8,128)(2,1)}, bf16[256,1024]{1,0:T(8,128)(2,1)S(1)}, u32[]{:S(2)}, u32[]{:S(2)}) %collective-permute-start.3) | collective-permute-done | bytes 524320 | tf_op jit(solution)/shard_map/ppermute | solution.py:14
  145.9 1.2 multiply_reduce_fusion.2
  147.1 0.3 fusion.22
  147.5 19.8 %collective-permute-done.7 = f32[256,1024]{1,0:T(8,128)S(1)} collective-permute-done((f32[256,1024]{1,0:T(8,128)S(1)}, f32[256,1024]{1,0:T(8,128)S(1)}, u32[]{:S(2)}, u32[]{:S(2)}) %collective-permute-start.7) | collective-permute-done | bytes 1048608 | tf_op jit(solution)/shard_map/ppermute | solution.py:14
  167.5 4.5 %collective-permute-start.8 = (f32[256,1024]{1,0:T(8,128)S(1)}, f32[256,1024]{1,0:T(8,128)S(1)}, u32[]{:S(2)}, u32[]{:S(2)}) collective-permute-start(f32[256,1024]{1,0:T(8,128)S(1)} %add.243), channel_id=1, source_target_pairs={{0,16},{4,20},{8,24},{12,28},{16,0},{20,4},{24,8},{28,12},{1,17},{... | collective-permute-start | bytes 3145736 | tf_op jit(solution)/shard_map/ppermute | solution.py:14
  172.0 1.4 convolution_add_fusion.2
  173.3 11.6 %fusion.63 = f32[3]{0:T(128)S(1)} fusion(f32[1]{0:T(128)} %bitcast.24, f32[1]{0:T(128)} %bitcast.23, f32[1]{0:T(128)} %bitcast.22, f32[1]{0:T(128)} %bitcast.27, f32[1]{0:T(128)} %bitcast.26, f32[1]{0:T(128)} %bitcast.25, f32[1]{0:T(128)} %bitcast.21, f32[1]{0:T(128)} %bitcast.20, f32[1]{0:T(128)} %bitcast.19, f32[1]{0:T(128)} %bitcast.18, f32[1]{0:T(128)} %bitcast.17, ...), kind=kLoop, calls=%fused_computation.151 | loop fusion | flops 51 | bytes 84 | tf_op jit(solution)/shard_map/add | solution.py:117
  184.9 0.5 multiply_reduce_fusion.1
  185.4 1.2 subtract_divide_fusion.1
  186.6 28.4 %collective-permute-done.8 = f32[256,1024]{1,0:T(8,128)S(1)} collective-permute-done((f32[256,1024]{1,0:T(8,128)S(1)}, f32[256,1024]{1,0:T(8,128)S(1)}, u32[]{:S(2)}, u32[]{:S(2)}) %collective-permute-start.8) | collective-permute-done | bytes 1048608 | tf_op jit(solution)/shard_map/ppermute | solution.py:14
  215.0 0.3 multiply_reduce_fusion
  215.3 0.4 fusion.12
  215.7 1.1 broadcast_multiply_fusion
  216.8 42.8 %all-reduce = (f32[1024]{0:T(1024)}, f32[3]{0:T(128)S(1)}) all-reduce(f32[1024]{0:T(1024)S(1)} %get-tuple-element.26, f32[3]{0:T(128)S(1)} %fusion.63), channel_id=1, replica_groups=mesh['dp'=8,'rep'=4] {'dp','rep'}, use_global_device_ids=true, to_apply=%region_12.13 | all-reduce | flops 1027 | bytes 8216 | tf_op jit(solution)/shard_map/psum | solution.py:134
  259.6 0.5 copy-done.7
  260.1 0.6 slice.14
  (36 shorter events, 1.2 us)
Async XLA Ops:
  1.6 21.7 %copy-start = (bf16[256,1024]{1,0:T(8,128)(2,1)S(1)}, bf16[256,1024]{1,0:T(8,128)(2,1)}, u32[]{:S(2)}) copy-start(bf16[256,1024]{1,0:T(8,128)(2,1)} %param.7) | copy-start | bytes 1572868
  19.4 3.9 %copy-start.2 = (f32[1024]{0:T(1024)S(1)}, f32[1024]{0:T(1024)}, u32[]{:S(2)}) copy-start(f32[1024]{0:T(1024)} %param.8) | copy-start | bytes 12292
  20.0 42.5 %all-to-all-start = ((s32[4,1,16]{2,1,0:T(1,128)}), s32[4,1,16]{2,1,0:T(1,128)S(1)}, u32[]{:S(2)}, u32[]{:S(2)}) async-start(s32[4,1,16]{2,1,0:T(1,128)} %bitcast.5), calls=%async_computation | async-start | bytes 4096 | tf_op jit(solution)/shard_map/all_to_all | solution.py:99
  23.5 1.0 copy-start.1
  23.7 38.9 %collective-permute-start = (bf16[256,1024]{1,0:T(8,128)(2,1)S(1)}, bf16[256,1024]{1,0:T(8,128)(2,1)}, u32[]{:S(2)}, u32[]{:S(2)}) collective-permute-start(bf16[256,1024]{1,0:T(8,128)(2,1)S(1)} %fusion.77), channel_id=1, source_target_pairs={{0,28},{4,0},{8,4},{12,8},{16,12},{20,16},{24,20},{28,24},{1,29},{... | collective-permute-start | bytes 1572872 | tf_op jit(solution)/shard_map/ppermute | solution.py:14
  28.9 36.8 %collective-permute-start.4 = (f32[256,1024]{1,0:T(8,128)}, f32[256,1024]{1,0:T(8,128)}, u32[]{:S(2)}, u32[]{:S(2)}) collective-permute-start(f32[256,1024]{1,0:T(8,128)} %fusion.33), channel_id=1, source_target_pairs={{0,28},{4,0},{8,4},{12,8},{16,12},{20,16},{24,20},{28,24},{1,29},{... | collective-permute-start | bytes 3145736 | tf_op jit(solution)/shard_map/ppermute | solution.py:14
  45.5 0.5 copy-start.5
  62.6 16.0 %collective-permute-start.1 = (bf16[256,1024]{1,0:T(8,128)(2,1)}, bf16[256,1024]{1,0:T(8,128)(2,1)}, u32[]{:S(2)}, u32[]{:S(2)}) collective-permute-start(bf16[256,1024]{1,0:T(8,128)(2,1)} %collective-permute-done), channel_id=1, source_target_pairs={{0,28},{4,0},{8,4},{12,8},{16,12},{20,16},{24,20},{28,24},{1,29},{... | collective-permute-start | bytes 1572872 | tf_op jit(solution)/shard_map/ppermute | solution.py:14
  68.3 32.9 %collective-permute-start.5 = (f32[256,1024]{1,0:T(8,128)}, f32[256,1024]{1,0:T(8,128)}, u32[]{:S(2)}, u32[]{:S(2)}) collective-permute-start(f32[256,1024]{1,0:T(8,128)} %convolution_add_fusion), channel_id=1, source_target_pairs={{0,28},{4,0},{8,4},{12,8},{16,12},{20,16},{24,20},{28,24},{1,29},{... | collective-permute-start | bytes 3145736 | tf_op jit(solution)/shard_map/ppermute | solution.py:14
  74.7 30.4 %all-to-all-start.1 = ((bf16[4,16,1024]{2,1,0:T(8,128)(2,1)}), bf16[4,16,1024]{2,1,0:T(8,128)(2,1)S(1)}, u32[]{:S(2)}, u32[]{:S(2)}) async-start(bf16[4,16,1024]{2,1,0:T(8,128)(2,1)} %broadcast_select_fusion), calls=%async_computation.1 | async-start | bytes 262144 | tf_op jit(solution)/shard_map/all_to_all | solution.py:101
  81.2 31.1 %collective-permute-start.2 = (bf16[256,1024]{1,0:T(8,128)(2,1)}, bf16[256,1024]{1,0:T(8,128)(2,1)}, u32[]{:S(2)}, u32[]{:S(2)}) collective-permute-start(bf16[256,1024]{1,0:T(8,128)(2,1)} %collective-permute-done.1), channel_id=1, source_target_pairs={{0,28},{4,0},{8,4},{12,8},{16,12},{20,16},{24,20},{28,24},{1,29},{... | collective-permute-start | bytes 1572872 | tf_op jit(solution)/shard_map/ppermute | solution.py:14
  103.4 1.7 copy-start.3
  103.4 1.7 copy-start.4
  103.4 31.4 %collective-permute-start.6 = (f32[256,1024]{1,0:T(8,128)}, f32[256,1024]{1,0:T(8,128)}, u32[]{:S(2)}, u32[]{:S(2)}) collective-permute-start(f32[256,1024]{1,0:T(8,128)} %add.241), channel_id=1, source_target_pairs={{0,28},{4,0},{8,4},{12,8},{16,12},{20,16},{24,20},{28,24},{1,29},{... | collective-permute-start | bytes 3145736 | tf_op jit(solution)/shard_map/ppermute | solution.py:14
  105.5 0.6 copy-start.6
  112.3 33.6 %collective-permute-start.3 = (bf16[256,1024]{1,0:T(8,128)(2,1)}, bf16[256,1024]{1,0:T(8,128)(2,1)S(1)}, u32[]{:S(2)}, u32[]{:S(2)}) collective-permute-start(bf16[256,1024]{1,0:T(8,128)(2,1)} %collective-permute-done.2), channel_id=1, source_target_pairs={{0,28},{4,0},{8,4},{12,8},{16,12},{20,16},{24,20},{28,24},{1,29},{... | collective-permute-start | bytes 1572872 | tf_op jit(solution)/shard_map/ppermute | solution.py:14
  136.2 31.1 %collective-permute-start.7 = (f32[256,1024]{1,0:T(8,128)S(1)}, f32[256,1024]{1,0:T(8,128)S(1)}, u32[]{:S(2)}, u32[]{:S(2)}) collective-permute-start(f32[256,1024]{1,0:T(8,128)S(1)} %add.242), channel_id=1, source_target_pairs={{0,28},{4,0},{8,4},{12,8},{16,12},{20,16},{24,20},{28,24},{1,29},{... | collective-permute-start | bytes 3145736 | tf_op jit(solution)/shard_map/ppermute | solution.py:14
  167.5 47.5 %collective-permute-start.8 = (f32[256,1024]{1,0:T(8,128)S(1)}, f32[256,1024]{1,0:T(8,128)S(1)}, u32[]{:S(2)}, u32[]{:S(2)}) collective-permute-start(f32[256,1024]{1,0:T(8,128)S(1)} %add.243), channel_id=1, source_target_pairs={{0,16},{4,20},{8,24},{12,28},{16,0},{20,4},{24,8},{28,12},{1,17},{... | collective-permute-start | bytes 3145736 | tf_op jit(solution)/shard_map/ppermute | solution.py:14
  259.6 0.5 copy-start.7
where the time goes:
time: 264 us; the launch traced here: 263 us
  waiting for transfers between devices  95.5 us (36%)
  local copies, waits for them, and re-layouts  52.1 us (20%)
  blocking collectives  42.8 us (16%)
  starting transfers between devices  24.7 us (9%)
  other arithmetic  23.6 us (9%)
  matrix products  19.7 us (7%)
  between operations  4.03 us (2%)
    ppermute x9, waiting for transfers between devices, shifted(): return lax.ppermute(value, axis, pairs)  95.5 us
    psum x1, blocking collectives, per_device(): gain_total, summary_total = lax.psum((gain_part, summary), ('dp', 'rep'))  42.8 us
    ppermute x9, starting transfers between devices, shifted(): return lax.ppermute(value, axis, pairs)  18.2 us
    scatter x1, local copies, waits for them, and re-layouts, per_device(): slot_pair = jnp.zeros((slot_total,), jnp.int32).at[target].set(jnp.arange...  16 us
    scatter x1, local copies, waits for them, and re-layouts, per_device(): asked_rows = jnp.zeros((slot_total,), jnp.int32).at[target].set(row_withi...  15.5 us
    scatter x1, local copies, waits for them, and re-layouts, per_device(): jnp.zeros((slot_total,), jnp.float32).at[target].set(1.0, mode='drop')  15.5 us
    add x1, other arithmetic, per_device(): summary + jnp.stack([jnp.sum(hard_weights * hard_products * multiplier),...  11.6 us
    dot_general x5, matrix products, score_tile(): lax.dot_general(circ_block, rec_block, (((1,), (1,)), ((), ())), preferre...  9.18 us
  transfers between devices with their start and end apart: 11, of which 7 were waited for; matrix products, arithmetic and copies ran while one was open for 27% of the time, Pallas kernels for 0%

commit v1 on v0

--- a/solution.py
+++ b/solution.py
@@ -131,7 +131,8 @@
     ) / rec_length
     grad_records = grad_pre * record_gain
     gain_part = jnp.sum(records.astype(jnp.float32) * grad_pre, axis=0)
-    gain_total, summary_total = lax.psum((gain_part, summary), ("dp", "rep"))
+    samples_wait = lambda s0: jax.lax.psum(jax.lax.psum(s0, "rep"), "dp")
+    gain_total, summary_total = samples_wait((gain_part, summary))
     pair_total = pair_rows * loop_count * rep_count
     statistics = jnp.stack([summary_total[0], summary_total[1]])
     mean_loss = jnp.stack([summary_total[2] / pair_total])

time: 264 us -> 252 us (0.955)
  the two profiles are of different devices: /device:TPU:12 before, /device:TPU:0 now
where the time goes in v1:
time: 252 us; the launch traced here: 251 us
  waiting for transfers between devices  93.2 us (37%)
  local copies, waits for them, and re-layouts  51.8 us (21%)
  starting transfers between devices  31.1 us (12%)
  blocking collectives  27.8 us (11%)
  other arithmetic  23.6 us (9%)
  matrix products  19.7 us (8%)
  between operations  4.02 us (2%)
    ppermute x9, waiting for transfers between devices, shifted(): return lax.ppermute(value, axis, pairs)  93.1 us
    psum x2, blocking collectives, per_device(): samples_wait = lambda s0: jax.lax.psum(jax.lax.psum(s0, 'rep'), 'dp')  27.8 us
    ppermute x9, starting transfers between devices, shifted(): return lax.ppermute(value, axis, pairs)  23.5 us
    scatter x1, local copies, waits for them, and re-layouts, per_device(): slot_pair = jnp.zeros((slot_total,), jnp.int32).at[target].set(jnp.arange...  16 us
    scatter x1, local copies, waits for them, and re-layouts, per_device(): asked_rows = jnp.zeros((slot_total,), jnp.int32).at[target].set(row_withi...  15.5 us
    scatter x1, local copies, waits for them, and re-layouts, per_device(): jnp.zeros((slot_total,), jnp.float32).at[target].set(1.0, mode='drop')  15.5 us
    add x1, other arithmetic, per_device(): summary + jnp.stack([jnp.sum(hard_weights * hard_products * multiplier),...  11.6 us
    dot_general x5, matrix products, score_tile(): lax.dot_general(circ_block, rec_block, (((1,), (1,)), ((), ())), preferre...  9.19 us
  transfers between devices with their start and end apart: 11, of which 7 were waited for; matrix products, arithmetic and copies ran while one was open for 29% of the time, Pallas kernels for 0%

profile of v1, /device:TPU:0, one launch (start us, length us, event | category | flops | bytes accessed | tf_op | source)
XLA Modules:
  0.0 251.2 jit_solution(9487909984934260542)
XLA Ops:
  0.6 0.8 copy.14
  1.9 1.2 reduce-window.6
  3.1 0.2 slice_reduce_fusion
  3.3 0.2 reduce-window.9
  3.9 15.5 %scatter_custom_fusion.2 = s32[64]{0:T(128)S(1)} fusion(s32[4096]{0:T(1024)S(1)} %bitcast.84, s32[4096]{0:T(1024)S(1)} %get-tuple-element.30, s32[]{:T(128)} %constant.87.clone.1), kind=kCustom, calls=%fused_computation.158 | custom fusion | bytes 260 | tf_op jit(solution)/shard_map/scatter | solution.py:89
  19.4 0.7 all_to_all.13
  20.0 4.2 %all-to-all-start = ((s32[4,1,16]{2,1,0:T(1,128)}), s32[4,1,16]{2,1,0:T(1,128)S(1)}, u32[]{:S(2)}, u32[]{:S(2)}) async-start(s32[4,1,16]{2,1,0:T(1,128)} %bitcast.5), calls=%async_computation | async-start | bytes 4096 | tf_op jit(solution)/shard_map/all_to_all | solution.py:99
  24.3 0.2 fusion.10
  24.7 5.1 %collective-permute-start = (bf16[256,1024]{1,0:T(8,128)(2,1)S(1)}, bf16[256,1024]{1,0:T(8,128)(2,1)}, u32[]{:S(2)}, u32[]{:S(2)}) collective-permute-start(bf16[256,1024]{1,0:T(8,128)(2,1)S(1)} %fusion.77), channel_id=1, source_target_pairs={{0,28},{4,0},{8,4},{12,8},{16,12},{20,16},{24,20},{28,24},{1,29},{... | collective-permute-start | bytes 1572872 | tf_op jit(solution)/shard_map/ppermute | solution.py:14
  29.8 0.2 fusion.11
  30.0 0.2 fusion.72
  31.5 1.2 multiply_reduce_fusion.6
  32.8 1.3 fusion.33
  34.1 0.8 collective-permute-start.4
  34.9 15.5 %scatter_custom_fusion.1 = f32[64]{0:T(128)S(1)} fusion(s32[4096]{0:T(1024)S(1)} %bitcast.85, f32[4096]{0:T(1024)S(1)} %broadcast.271, f32[]{:T(128)} %constant.85.clone.1), kind=kCustom, calls=%fused_computation.156 | custom fusion | bytes 260 | tf_op jit(solution)/shard_map/scatter | solution.py:97
  50.4 0.3 fusion.35
  50.7 0.2 copy-done.5
  50.9 0.5 broadcast_compare_fusion.2
  51.4 16.0 %scatter_custom_fusion = s32[64]{0:T(128)} fusion(s32[4096]{0:T(1024)S(1)} %bitcast.86, s32[4096]{0:T(1024)S(1)} %add_select_fusion.1, s32[]{:T(128)} %constant.87.clone.1), kind=kCustom, calls=%fused_computation.160 | custom fusion | bytes 260 | tf_op jit(solution)/shard_map/scatter | solution.py:95
  67.5 1.1 collective-permute-start.1
  68.6 2.3 multiply_reduce_fusion.5
  70.9 2.5 %convolution_add_fusion = f32[256,1024]{1,0:T(8,128)} fusion(f32[256,1024]{1,0:T(8,128)} %collective-permute-done.4, bf16[256,1024]{1,0:T(8,128)(2,1)S(1)} %fusion.72, f32[256,256]{1,0:T(8,128)S(1)} %get-tuple-element.37), kind=kOutput, calls=%fused_computation.4 | convolution fusion | flops 134742016 | bytes 2883584 | tf_op jit(solution)/shard_map/dot_general | solution.py:24
  73.5 0.8 collective-permute-start.5
  74.3 0.6 pad_clamp_fusion
  74.9 0.8 gather_fusion
  75.7 0.7 broadcast_select_fusion
  76.4 3.3 %all-to-all-start.1 = ((bf16[4,16,1024]{2,1,0:T(8,128)(2,1)}), bf16[4,16,1024]{2,1,0:T(8,128)(2,1)S(1)}, u32[]{:S(2)}, u32[]{:S(2)}) async-start(bf16[4,16,1024]{2,1,0:T(8,128)(2,1)} %broadcast_select_fusion), calls=%async_computation.1 | async-start | bytes 262144 | tf_op jit(solution)/shard_map/all_to_all | solution.py:101
  79.8 2.8 %collective-permute-done.1 = bf16[256,1024]{1,0:T(8,128)(2,1)} collective-permute-done((bf16[256,1024]{1,0:T(8,128)(2,1)}, bf16[256,1024]{1,0:T(8,128)(2,1)}, u32[]{:S(2)}, u32[]{:S(2)}) %collective-permute-start.1) | collective-permute-done | bytes 524320 | tf_op jit(solution)/shard_map/ppermute | solution.py:14
  82.6 2.3 multiply_reduce_fusion.4
  84.8 0.3 fusion.28
  85.2 3.9 %collective-permute-start.2 = (bf16[256,1024]{1,0:T(8,128)(2,1)}, bf16[256,1024]{1,0:T(8,128)(2,1)}, u32[]{:S(2)}, u32[]{:S(2)}) collective-permute-start(bf16[256,1024]{1,0:T(8,128)(2,1)} %collective-permute-done.1), channel_id=1, source_target_pairs={{0,28},{4,0},{8,4},{12,8},{16,12},{20,16},{24,20},{28,24},{1,29},{... | collective-permute-start | bytes 1572872 | tf_op jit(solution)/shard_map/ppermute | solution.py:14
  89.1 16.0 %collective-permute-done.5 = f32[256,1024]{1,0:T(8,128)} collective-permute-done((f32[256,1024]{1,0:T(8,128)}, f32[256,1024]{1,0:T(8,128)}, u32[]{:S(2)}, u32[]{:S(2)}) %collective-permute-start.5) | collective-permute-done | bytes 1048608 | tf_op jit(solution)/shard_map/ppermute | solution.py:14
  105.1 2.3 add.245
  107.4 3.8 %collective-permute-start.6 = (f32[256,1024]{1,0:T(8,128)}, f32[256,1024]{1,0:T(8,128)}, u32[]{:S(2)}, u32[]{:S(2)}) collective-permute-start(f32[256,1024]{1,0:T(8,128)} %add.245), channel_id=1, source_target_pairs={{0,28},{4,0},{8,4},{12,8},{16,12},{20,16},{24,20},{28,24},{1,29},{... | collective-permute-start | bytes 3145736 | tf_op jit(solution)/shard_map/ppermute | solution.py:14
  111.3 0.4 fusion.9
  111.6 0.6 copy-done.6
  112.3 0.6 multiply_reduce_fusion.7
  112.9 0.4 fusion.42
  113.3 3.0 %collective-permute-done.2 = bf16[256,1024]{1,0:T(8,128)(2,1)} collective-permute-done((bf16[256,1024]{1,0:T(8,128)(2,1)}, bf16[256,1024]{1,0:T(8,128)(2,1)}, u32[]{:S(2)}, u32[]{:S(2)}) %collective-permute-start.2) | collective-permute-done | bytes 524320 | tf_op jit(solution)/shard_map/ppermute | solution.py:14
  116.3 3.8 %collective-permute-start.3 = (bf16[256,1024]{1,0:T(8,128)(2,1)}, bf16[256,1024]{1,0:T(8,128)(2,1)S(1)}, u32[]{:S(2)}, u32[]{:S(2)}) collective-permute-start(bf16[256,1024]{1,0:T(8,128)(2,1)} %collective-permute-done.2), channel_id=1, source_target_pairs={{0,28},{4,0},{8,4},{12,8},{16,12},{20,16},{24,20},{28,24},{1,29},{... | collective-permute-start | bytes 1572872 | tf_op jit(solution)/shard_map/ppermute | solution.py:14
  120.1 2.2 multiply_reduce_fusion.3
  122.4 0.3 fusion.25
  122.7 16.0 %collective-permute-done.6 = f32[256,1024]{1,0:T(8,128)} collective-permute-done((f32[256,1024]{1,0:T(8,128)}, f32[256,1024]{1,0:T(8,128)}, u32[]{:S(2)}, u32[]{:S(2)}) %collective-permute-start.6) | collective-permute-done | bytes 1048608 | tf_op jit(solution)/shard_map/ppermute | solution.py:14
  138.8 1.4 add.246
  140.1 4.1 %collective-permute-start.7 = (f32[256,1024]{1,0:T(8,128)S(1)}, f32[256,1024]{1,0:T(8,128)S(1)}, u32[]{:S(2)}, u32[]{:S(2)}) collective-permute-start(f32[256,1024]{1,0:T(8,128)S(1)} %add.246), channel_id=1, source_target_pairs={{0,28},{4,0},{8,4},{12,8},{16,12},{20,16},{24,20},{28,24},{1,29},{... | collective-permute-start | bytes 3145736 | tf_op jit(solution)/shard_map/ppermute | solution.py:14
  144.2 1.4 convolution_add_fusion.4
  145.6 1.4 convolution_add_fusion.3
  146.9 3.0 %collective-permute-done.3 = bf16[256,1024]{1,0:T(8,128)(2,1)S(1)} collective-permute-done((bf16[256,1024]{1,0:T(8,128)(2,1)}, bf16[256,1024]{1,0:T(8,128)(2,1)S(1)}, u32[]{:S(2)}, u32[]{:S(2)}) %collective-permute-start.3) | collective-permute-done | bytes 524320 | tf_op jit(solution)/shard_map/ppermute | solution.py:14
  149.9 1.2 multiply_reduce_fusion.2
  151.1 0.3 fusion.22
  151.4 20.2 %collective-permute-done.7 = f32[256,1024]{1,0:T(8,128)S(1)} collective-permute-done((f32[256,1024]{1,0:T(8,128)S(1)}, f32[256,1024]{1,0:T(8,128)S(1)}, u32[]{:S(2)}, u32[]{:S(2)}) %collective-permute-start.7) | collective-permute-done | bytes 1048608 | tf_op jit(solution)/shard_map/ppermute | solution.py:14
  171.6 0.2 add.247
  171.9 1.4 convolution_add_fusion.2
  173.2 11.6 %fusion.63 = f32[3]{0:T(128)S(1)} fusion(f32[1]{0:T(128)} %bitcast.24, f32[1]{0:T(128)} %bitcast.23, f32[1]{0:T(128)} %bitcast.22, f32[1]{0:T(128)} %bitcast.27, f32[1]{0:T(128)} %bitcast.26, f32[1]{0:T(128)} %bitcast.25, f32[1]{0:T(128)} %bitcast.21, f32[1]{0:T(128)} %bitcast.20, f32[1]{0:T(128)} %bitcast.19, f32[1]{0:T(128)} %bitcast.18, f32[1]{0:T(128)} %bitcast.17, ...), kind=kLoop, calls=%fused_computation.151 | loop fusion | flops 51 | bytes 84 | tf_op jit(solution)/shard_map/add | solution.py:117
  184.8 0.5 multiply_reduce_fusion.1
  185.3 1.2 subtract_divide_fusion.1
  186.5 32.2 %collective-permute-done.8 = f32[256,1024]{1,0:T(8,128)S(1)} collective-permute-done((f32[256,1024]{1,0:T(8,128)S(1)}, f32[256,1024]{1,0:T(8,128)S(1)}, u32[]{:S(2)}, u32[]{:S(2)}) %collective-permute-start.8) | collective-permute-done | bytes 1048608 | tf_op jit(solution)/shard_map/ppermute | solution.py:14
  218.7 0.3 multiply_reduce_fusion
  219.0 0.4 fusion.12
  219.4 1.1 broadcast_multiply_fusion
  220.5 6.8 %all-reduce.1 = (f32[1024]{0:T(1024)S(1)}, f32[3]{0:T(128)S(1)}) all-reduce(f32[1024]{0:T(1024)S(1)} %get-tuple-element.28, f32[3]{0:T(128)S(1)} %fusion.63), channel_id=1, replica_groups=mesh['dp'=8,'rep'=4] {'rep'}, use_global_device_ids=true, to_apply=%region_12.13 | all-reduce | flops 1027 | bytes 8216 | tf_op jit(solution)/shard_map/psum | solution.py:134
  227.3 21.0 %all-reduce = (f32[1024]{0:T(1024)}, f32[3]{0:T(128)S(1)}) all-reduce(f32[1024]{0:T(1024)S(1)} %get-tuple-element.25, f32[3]{0:T(128)S(1)} %get-tuple-element.26), channel_id=1, replica_groups=mesh['dp'=8,'rep'=4] {'dp'}, use_global_device_ids=true, to_apply=%region_13.14 | all-reduce | flops 1027 | bytes 8216 | tf_op jit(solution)/shard_map/psum | solution.py:134
  248.3 0.5 copy-done.7
  248.8 0.6 slice.14
  (37 shorter events, 1.1 us)
Async XLA Ops:
  1.6 22.7 %copy-start = (bf16[256,1024]{1,0:T(8,128)(2,1)S(1)}, bf16[256,1024]{1,0:T(8,128)(2,1)}, u32[]{:S(2)}) copy-start(bf16[256,1024]{1,0:T(8,128)(2,1)} %param.7) | copy-start | bytes 1572868
  19.4 4.9 %copy-start.2 = (f32[1024]{0:T(1024)S(1)}, f32[1024]{0:T(1024)}, u32[]{:S(2)}) copy-start(f32[1024]{0:T(1024)} %param.8) | copy-start | bytes 12292
  20.0 47.4 %all-to-all-start = ((s32[4,1,16]{2,1,0:T(1,128)}), s32[4,1,16]{2,1,0:T(1,128)S(1)}, u32[]{:S(2)}, u32[]{:S(2)}) async-start(s32[4,1,16]{2,1,0:T(1,128)} %bitcast.5), calls=%async_computation | async-start | bytes 4096 | tf_op jit(solution)/shard_map/all_to_all | solution.py:99
  24.5 5.3 %copy-start.1 = (bf16[256,1024]{1,0:T(8,128)(2,1)S(1)}, bf16[256,1024]{1,0:T(8,128)(2,1)}, u32[]{:S(2)}) copy-start(bf16[256,1024]{1,0:T(8,128)(2,1)} %param.6) | copy-start | bytes 1572868
  24.7 42.8 %collective-permute-start = (bf16[256,1024]{1,0:T(8,128)(2,1)S(1)}, bf16[256,1024]{1,0:T(8,128)(2,1)}, u32[]{:S(2)}, u32[]{:S(2)}) collective-permute-start(bf16[256,1024]{1,0:T(8,128)(2,1)S(1)} %fusion.77), channel_id=1, source_target_pairs={{0,28},{4,0},{8,4},{12,8},{16,12},{20,16},{24,20},{28,24},{1,29},{... | collective-permute-start | bytes 1572872 | tf_op jit(solution)/shard_map/ppermute | solution.py:14
  34.1 36.8 %collective-permute-start.4 = (f32[256,1024]{1,0:T(8,128)}, f32[256,1024]{1,0:T(8,128)}, u32[]{:S(2)}, u32[]{:S(2)}) collective-permute-start(f32[256,1024]{1,0:T(8,128)} %fusion.33), channel_id=1, source_target_pairs={{0,28},{4,0},{8,4},{12,8},{16,12},{20,16},{24,20},{28,24},{1,29},{... | collective-permute-start | bytes 3145736 | tf_op jit(solution)/shard_map/ppermute | solution.py:14
  50.4 0.5 copy-start.5
  67.5 15.1 %collective-permute-start.1 = (bf16[256,1024]{1,0:T(8,128)(2,1)}, bf16[256,1024]{1,0:T(8,128)(2,1)}, u32[]{:S(2)}, u32[]{:S(2)}) collective-permute-start(bf16[256,1024]{1,0:T(8,128)(2,1)} %collective-permute-done), channel_id=1, source_target_pairs={{0,28},{4,0},{8,4},{12,8},{16,12},{20,16},{24,20},{28,24},{1,29},{... | collective-permute-start | bytes 1572872 | tf_op jit(solution)/shard_map/ppermute | solution.py:14
  73.5 31.6 %collective-permute-start.5 = (f32[256,1024]{1,0:T(8,128)}, f32[256,1024]{1,0:T(8,128)}, u32[]{:S(2)}, u32[]{:S(2)}) collective-permute-start(f32[256,1024]{1,0:T(8,128)} %convolution_add_fusion), channel_id=1, source_target_pairs={{0,28},{4,0},{8,4},{12,8},{16,12},{20,16},{24,20},{28,24},{1,29},{... | collective-permute-start | bytes 3145736 | tf_op jit(solution)/shard_map/ppermute | solution.py:14
  76.4 34.8 %all-to-all-start.1 = ((bf16[4,16,1024]{2,1,0:T(8,128)(2,1)}), bf16[4,16,1024]{2,1,0:T(8,128)(2,1)S(1)}, u32[]{:S(2)}, u32[]{:S(2)}) async-start(bf16[4,16,1024]{2,1,0:T(8,128)(2,1)} %broadcast_select_fusion), calls=%async_computation.1 | async-start | bytes 262144 | tf_op jit(solution)/shard_map/all_to_all | solution.py:101
  85.2 31.1 %collective-permute-start.2 = (bf16[256,1024]{1,0:T(8,128)(2,1)}, bf16[256,1024]{1,0:T(8,128)(2,1)}, u32[]{:S(2)}, u32[]{:S(2)}) collective-permute-start(bf16[256,1024]{1,0:T(8,128)(2,1)} %collective-permute-done.1), channel_id=1, source_target_pairs={{0,28},{4,0},{8,4},{12,8},{16,12},{20,16},{24,20},{28,24},{1,29},{... | collective-permute-start | bytes 1572872 | tf_op jit(solution)/shard_map/ppermute | solution.py:14
  107.4 3.9 %copy-start.3 = (pred[64]{0:T(512)(128)(4,1)S(1)}, pred[64]{0:T(512)(128)(4,1)}, u32[]{:S(2)}) copy-start(pred[64]{0:T(512)(128)(4,1)} %broadcast_compare_fusion.2) | copy-start | bytes 196
  107.4 3.9 %copy-start.4 = (s32[64]{0:T(128)S(1)}, s32[64]{0:T(128)}, u32[]{:S(2)}) copy-start(s32[64]{0:T(128)} %scatter_custom_fusion) | copy-start | bytes 772
  107.4 31.4 %collective-permute-start.6 = (f32[256,1024]{1,0:T(8,128)}, f32[256,1024]{1,0:T(8,128)}, u32[]{:S(2)}, u32[]{:S(2)}) collective-permute-start(f32[256,1024]{1,0:T(8,128)} %add.245), channel_id=1, source_target_pairs={{0,28},{4,0},{8,4},{12,8},{16,12},{20,16},{24,20},{28,24},{1,29},{... | collective-permute-start | bytes 3145736 | tf_op jit(solution)/shard_map/ppermute | solution.py:14
  111.6 0.6 copy-start.6
  116.3 33.6 %collective-permute-start.3 = (bf16[256,1024]{1,0:T(8,128)(2,1)}, bf16[256,1024]{1,0:T(8,128)(2,1)S(1)}, u32[]{:S(2)}, u32[]{:S(2)}) collective-permute-start(bf16[256,1024]{1,0:T(8,128)(2,1)} %collective-permute-done.2), channel_id=1, source_target_pairs={{0,28},{4,0},{8,4},{12,8},{16,12},{20,16},{24,20},{28,24},{1,29},{... | collective-permute-start | bytes 1572872 | tf_op jit(solution)/shard_map/ppermute | solution.py:14
  140.1 31.5 %collective-permute-start.7 = (f32[256,1024]{1,0:T(8,128)S(1)}, f32[256,1024]{1,0:T(8,128)S(1)}, u32[]{:S(2)}, u32[]{:S(2)}) collective-permute-start(f32[256,1024]{1,0:T(8,128)S(1)} %add.246), channel_id=1, source_target_pairs={{0,28},{4,0},{8,4},{12,8},{16,12},{20,16},{24,20},{28,24},{1,29},{... | collective-permute-start | bytes 3145736 | tf_op jit(solution)/shard_map/ppermute | solution.py:14
  171.8 46.9 %collective-permute-start.8 = (f32[256,1024]{1,0:T(8,128)S(1)}, f32[256,1024]{1,0:T(8,128)S(1)}, u32[]{:S(2)}, u32[]{:S(2)}) collective-permute-start(f32[256,1024]{1,0:T(8,128)S(1)} %add.247), channel_id=1, source_target_pairs={{0,16},{4,20},{8,24},{12,28},{16,0},{20,4},{24,8},{28,12},{1,17},{... | collective-permute-start | bytes 3145736 | tf_op jit(solution)/shard_map/ppermute | solution.py:14
  248.3 0.5 copy-start.7
